TPU v7x, 32 devices: a whole 2x2x4 slice. The times are simulated.
32 devices in a mesh: groups: 2 (over y), frame: 8 (over z, x), row: 2 (over core).
Axes of the slice: x: 2, y: 2, z: 4, core: 2. Of those that a mesh axis runs over, the one named last changes fastest.
Arguments:
- latent: bfloat16 [16, 16, 64, 640], P(('groups', 'frame'), 'row'), parts along dimension 0, may hold values from -18 to 18
- norm_gain: float32 [640], replicated, may hold values from 0.1 to 1.9
- time_kernel: bfloat16 [3, 640, 640], replicated, may hold values from -0.125 to 0.125
- space_norm: float32 [640], replicated, may hold values from 0.1 to 1.9
- space_qkv: bfloat16 [640, 1920], replicated, may hold values from -12 to 12
- space_out: bfloat16 [640, 640], replicated, may hold values from -0.25 to 0.25
- time_norm: float32 [640], replicated, may hold values from 0.1 to 1.9
- time_qkv: bfloat16 [640, 1920], replicated, may hold values from -12 to 12
- time_out: bfloat16 [640, 640], replicated, may hold values from -0.25 to 0.25
Outputs:
- output: float32 [16, 16, 64, 640], P(('groups', 'frame'), 'row'), parts along dimension 0
There are 2 independent parts, one for each index of `groups`. A program takes and returns all parts, laid end to end along the dimension named above; an argument that names none is the same for every part. Nothing has to cross between parts.
All inputs are finite; a program needn't handle non-finite values.
Results may differ from a plain program's by a relative error of at most 0.0018.
Values may be sent and summed in bfloat16 or wider, within the bound.
A program may use at most 128 MiB of HBM per device.

v0:
```python
import jax
import jax.numpy as jnp
from jax import lax
from jax.sharding import PartitionSpec as P

HEADS = 10
GROUPS = 32
epsilon = 1e-05


def padded_2(block, sides, width):
    for axis, dim in sides:
        count = lax.axis_size(axis)
        forward = [(i, i + 1) for i in range(count - 1)]
        backward = [(target, source) for source, target in forward]
        low = lax.ppermute(
            lax.slice_in_dim(block, block.shape[dim] - width, None, axis=dim), axis, forward
        )
        high = lax.ppermute(lax.slice_in_dim(block, 0, width, axis=dim), axis, backward)
        block = jnp.concatenate([low, block, high], axis=dim)
    return block


def normalize_silu(grouped, first, second, number, gain, shape):
    center = first / number
    spread = second / number - center * center
    scaling = lax.rsqrt(spread + epsilon)
    normed = ((grouped - center[:, None]) * scaling[:, None]).reshape(shape) * gain
    return jax.nn.silu(normed).astype(jnp.bfloat16)


def layer_norm(inputs, gain):
    center = jnp.mean(inputs, axis=-1, keepdims=True)
    shifted = inputs - center
    spread = jnp.mean(shifted * shifted, axis=-1, keepdims=True)
    return (shifted * lax.rsqrt(spread + epsilon) * gain).astype(jnp.bfloat16)


def project_three(inputs, weight):
    channels = weight.shape[0]
    lead = inputs.shape[:-1]
    packed = jnp.dot(
        inputs.reshape(-1, channels), weight, preferred_element_type=jnp.float32
    ).astype(jnp.bfloat16)
    packed = packed.reshape(lead + (3 * channels,))
    return (
        packed[..., :channels],
        packed[..., channels : 2 * channels],
        packed[..., 2 * channels :],
    )


def time_attend(queries, key_rows, values):
    frames, pixels, channels = queries.shape
    head_size = channels // HEADS
    query_heads = queries.reshape(frames, pixels, HEADS, head_size)
    key_heads = key_rows.reshape(frames, pixels, HEADS, head_size)
    value_heads = values.reshape(frames, pixels, HEADS, head_size)
    scores = jnp.einsum(
        "qphd,kphd->phqk", query_heads, key_heads, preferred_element_type=jnp.float32
    ) * head_size ** (-0.5)
    raised = jnp.exp(scores - jnp.max(scores, axis=-1, keepdims=True))
    weight_sum = jnp.sum(raised, axis=-1)
    weights = raised.astype(jnp.bfloat16)
    result = jnp.einsum("phqk,kphd->qphd", weights, value_heads, preferred_element_type=jnp.float32)
    result = result / jnp.transpose(weight_sum, (2, 0, 1))[:, :, :, None]
    return result.astype(jnp.bfloat16).reshape(frames, pixels, channels)


def add_projected(base, attended, weight):
    channels = weight.shape[0]
    summed = base.reshape(-1, channels) + jnp.dot(
        attended.reshape(-1, channels), weight, preferred_element_type=jnp.float32
    )
    return summed.reshape(base.shape)


def body(
    latent, norm_gain, time_kernel, space_norm, space_qkv, space_out, time_norm, time_qkv, time_out
):
    frames, row_count, col_count, channels = latent.shape
    pixels = row_count * col_count
    per_group = channels // GROUPS
    head_size = channels // HEADS
    grouped = latent.astype(jnp.float32).reshape(frames, row_count, col_count, GROUPS, per_group)
    first = jnp.sum(grouped, axis=(0, 1, 2, 4))
    second = jnp.sum(grouped * grouped, axis=(0, 1, 2, 4))
    first, second = lax.psum((first, second), ("frame", "row"))
    number = frames * lax.axis_size("frame") * pixels * lax.axis_size("row") * per_group
    wide = padded_2(latent, (("frame", 0),), 1)
    wide_frames = wide.shape[0]
    wide_grouped = wide.astype(jnp.float32).reshape(
        wide_frames, row_count, col_count, GROUPS, per_group
    )
    padded = normalize_silu(wide_grouped, first, second, number, norm_gain, wide.shape)
    me, count = (lax.axis_index("frame"), lax.axis_size("frame"))
    place = me * frames - 1 + jnp.arange(wide_frames)
    inside = (place >= 0) & (place < count * frames)
    padded = jnp.where(inside[:, None, None, None], padded, jnp.zeros((), padded.dtype))
    mixed = jnp.zeros((frames * pixels, channels), jnp.float32)
    for tap in range(3):
        window = padded[tap : tap + frames].reshape(-1, channels)
        mixed = mixed + jnp.dot(window, time_kernel[tap], preferred_element_type=jnp.float32)
    stepped = latent.astype(jnp.float32).reshape(-1, channels) + mixed
    stepped = stepped.reshape(frames, pixels, channels)
    tokens = layer_norm(stepped, space_norm)
    queries, key_rows, values = project_three(tokens, space_qkv)
    query_heads = queries.reshape(frames, pixels, HEADS, head_size)
    top_score = jnp.full((frames, HEADS, pixels), -jnp.inf, jnp.float32)
    weight_sum = jnp.zeros((frames, HEADS, pixels), jnp.float32)
    partial_sum = jnp.zeros((frames, HEADS, pixels, head_size), jnp.float32)
    key_piece = lax.all_gather(key_rows, "row", axis=1, tiled=True)
    value_piece = lax.all_gather(values, "row", axis=1, tiled=True)
    key_count = key_piece.shape[1]
    key_heads = key_piece.reshape(frames, key_count, HEADS, head_size)
    value_heads = value_piece.reshape(frames, key_count, HEADS, head_size)
    scores = jnp.einsum(
        "fqhd,fkhd->fhqk", query_heads, key_heads, preferred_element_type=jnp.float32
    ) * head_size ** (-0.5)
    new_top = jnp.max(scores, axis=-1)
    rescale = jnp.exp(top_score - new_top)
    raised = jnp.exp(scores - new_top[..., None])
    weight_sum = weight_sum * rescale + jnp.sum(raised, axis=-1)
    weights = raised.astype(jnp.bfloat16)
    partial_sum = partial_sum * rescale[..., None] + jnp.einsum(
        "fhqk,fkhd->fhqd", weights, value_heads, preferred_element_type=jnp.float32
    )
    top_score, weight_sum, partial_sum = (new_top, weight_sum, partial_sum)
    attended = (partial_sum / weight_sum[..., None]).astype(jnp.bfloat16)
    attended = jnp.transpose(attended, (0, 2, 1, 3)).reshape(frames, pixels, channels)
    spaced = add_projected(stepped, attended, space_out)
    normed = layer_norm(spaced, time_norm)
    moved = lax.all_to_all(normed, "frame", split_axis=1, concat_axis=0, tiled=True)
    queries, key_rows, values = project_three(moved, time_qkv)
    result = time_attend(queries, key_rows, values)
    result = lax.all_to_all(result, "frame", split_axis=0, concat_axis=1, tiled=True)
    output = add_projected(spaced, result, time_out)
    return output.reshape(frames, row_count, col_count, channels)


def solution(mesh):
    return jax.shard_map(
        body,
        mesh=mesh,
        in_specs=(
            P(("groups", "frame"), "row", None, None),
            P(),
            P(),
            P(),
            P(),
            P(),
            P(),
            P(),
            P(),
        ),
        out_specs=P(("groups", "frame"), "row", None, None),
        check_vma=False,
    )
```

profile of v0, /device:TPU:0, one launch (start us, length us, event | category | flops | bytes accessed | tf_op | source)
XLA Modules:
  0.0 192.2 jit_solution(7589339824454949340)
XLA Ops:
  6.5 5.0 %collective-permute-start = (bf16[1,8,64,640]{3,2,1,0:T(8,128)(2,1)}, bf16[1,8,64,640]{3,2,1,0:T(8,128)(2,1)S(1)}, u32[]{:S(2)}, u32[]{:S(2)}) collective-permute-start(bf16[1,8,64,640]{3,2,1,0:T(8,128)(2,1)} %param.9), channel_id=1, source_target_pairs={{0,2},{2,4},{4,6},{6,8},{8,10},{10,12},{12,14},{1,3},{3,5},{5,7},{... | collective-permute-start | bytes 1966088 | tf_op jit(solution)/shard_map/ppermute | solution.py:16
  11.6 1.3 collective-permute-start.1
  12.9 1.3 convert_reduce_fusion
  14.6 49.5 %all-reduce = (f32[32]{0:T(128)S(1)}, f32[32]{0:T(128)S(1)}) all-reduce(f32[32]{0:T(128)S(1)} %reduce_sum.91, f32[32]{0:T(128)S(1)} %reduce_sum.88), channel_id=1, replica_groups=mesh['groups'=2,'frame'=8,'row'=2] {'frame','row'}, use_global_device_ids=true, to_apply=%region_5.6 | all-reduce | flops 64 | bytes 512 | tf_op jit(solution)/shard_map/psum | solution.py:88
  64.5 2.5 %fusion.8 = bf16[3,8,64,640]{3,2,1,0:T(8,128)(2,1)S(1)} fusion(bf16[1,8,64,640]{3,2,1,0:T(8,128)(2,1)} %collective-permute-done.1, bf16[1,8,64,640]{3,2,1,0:T(8,128)(2,1)} %param.9, bf16[1,8,64,640]{3,2,1,0:T(8,128)(2,1)S(1)} %collective-permute-done, f32[640]{0:T(1024)} %param.10, f32[640]{0:T(1024)S(1)} %mul.99, f32[640]{0:T(1024)S(1)} %sub.69, ...), kind=kLoop, calls=%fused_computation.15 | loop fusion | flops 11796480 | bytes 3939843 | tf_op jit(solution)/shard_map/jit(_where)/select_n | solution.py:99
  67.1 0.2 fusion.38
  67.3 1.5 copy-done.7
  68.7 0.7 fusion.19
  69.5 0.7 fusion.21
  70.3 0.3 copy-done.6
  70.6 0.9 fusion.39
  71.5 0.3 multiply_reduce_fusion.3
  71.9 1.9 fusion.4
  73.8 1.2 fusion.37
  75.0 0.2 all-gather.5.cloned.1.call-start
  75.2 0.3 copy.50
  75.5 0.3 all-gather.5.cloned.1.call-update
  75.8 6.1 %all-gather.3.cloned.1.call-done = bf16[1,1024,640]{2,1,0:T(8,128)(2,1)} async-done(((bf16[1,512,640]{2,1,0:T(8,128)(2,1)}), bf16[1,1024,640]{2,1,0:T(8,128)(2,1)}) %all-gather.3.cloned.1.call-update) | async-done | bytes 1310736 | tf_op jit(solution)/shard_map/all_gather | solution.py:112
  81.9 1.6 copy.51
  83.5 3.0 %multiply_reduce_fusion = (f32[10,512]{1,0:T(8,128)S(1)}, f32[10,512,1024]{2,1,0:T(8,128)S(1)}) fusion(bf16[512,10,64]{0,2,1:T(8,128)(2,1)S(1)} %bitcast.69, bf16[1024,10,64]{0,2,1:T(8,128)(2,1)S(1)} %bitcast.63), kind=kOutput, calls=%fused_computation.1 | convolution fusion | flops 681569280 | bytes 22958080 | tf_op jit(solution)/shard_map/fqhd,fkhd->fhqk/dot_general | solution.py:117
  86.5 4.6 %fusion = f32[10,512]{1,0:T(8,128)S(1)} fusion(f32[10,512,1024]{2,1,0:T(8,128)S(1)} %get-tuple-element.25, f32[10,512]{1,0:T(8,128)S(1)} %get-tuple-element.24), kind=kLoop, calls=%fused_computation.2 | loop fusion | flops 15723520 | bytes 21012480 | tf_op jit(solution)/shard_map/reduce_sum | solution.py:123
  91.1 3.0 %copy-done.2 = f32[10,512,1024]{2,1,0:T(8,128)} copy-done((f32[10,512,1024]{2,1,0:T(8,128)}, f32[10,512,1024]{2,1,0:T(8,128)S(1)}, u32[]{:S(2)}) %copy-start.2) | copy-done | bytes 20971544
  94.1 1.6 copy.52
  95.8 9.4 %divide_convert_fusion = bf16[10,512,64]{1,2,0:T(8,128)(2,1)S(1)} fusion(bf16[1024,10,64]{0,2,1:T(8,128)(2,1)S(1)} %bitcast.75, f32[10,512,1024]{2,1,0:T(8,128)} %copy-done.2, f32[10,512]{1,0:T(8,128)S(1)} %get-tuple-element.24, f32[10,512]{1,0:T(8,128)S(1)} %get-tuple-element.19, f32[10,512]{1,0:T(8,128)S(1)} %get-tuple-element.18), kind=kOutput, calls=%fused_computation.26 | convolution fusion | flops 687800320 | bytes 22999040 | tf_op jit(solution)/shard_map/fhqk,fkhd->fhqd/dot_general | solution.py:125
  105.2 0.9 fusion.40
  106.1 0.3 multiply_reduce_fusion.2
  106.4 0.2 fusion.27
  106.6 2.1 %copy.73 = bf16[1,512,640]{2,0,1:T(2,128)(2,1)} copy(bf16[1,512,640]{2,1,0:T(8,128)(2,1)S(1)} %fusion.27) | data formatting | bytes 1310720 | tf_op jit(solution)/shard_map/convert_element_type | solution.py:36
  108.7 0.5 broadcast.133
  109.3 5.6 %reduce.17 = bf16[512,640]{1,0:T(8,128)(2,1)S(1)} reduce(bf16[512,1,640]{2,1,0:T(2,128)(2,1)} %bitcast.64, bf16[]{:T(256)} %broadcast.133), dimensions={1}, to_apply=%bitcast.61.reduce_sub_computation | reduce | bytes 1310722
  114.8 0.2 reshape.213
  115.0 23.7 %all_to_all.8 = bf16[8,2,20480]{2,1,0:T(2,128)(2,1)S(1)} all-to-all(bf16[8,2,20480]{2,1,0:T(2,128)(2,1)S(1)} %reshape.213), channel_id=1, replica_groups=mesh['groups'=2,'frame'=8,'row'=2] {'frame'}, dimensions={0} | all-to-all | bytes 1310720 | tf_op jit(solution)/shard_map/all_to_all | solution.py:133
  138.7 0.6 reshape.214
  139.4 3.4 %convolution_convert_fusion = bf16[512,1920]{1,0:T(8,128)(2,1)S(1)} fusion(bf16[640,1920]{1,0:T(8,128)(2,1)} %param.16, bf16[1,512,640]{2,0,1:T(2,128)(2,1)S(1)} %bitcast.76), kind=kOutput, calls=%fused_computation.6 | convolution fusion | flops 1259274240 | bytes 5079040 | tf_op jit(solution)/shard_map/dot_general | solution.py:42
  142.8 1.1 fusion.36
  143.9 1.6 copy.66
  145.6 1.7 copy.57
  147.3 0.8 copy.67
  148.0 1.6 copy.58
  149.6 0.8 copy.65
  150.4 1.7 copy.59
  152.1 2.8 %multiply_reduce_fusion.1 = (f32[64,10,8]{2,1,0:T(8,128)S(1)}, f32[64,10,8,8]{2,3,1,0:T(8,128)S(1)}) fusion(bf16[8,64,10,64]{3,0,2,1:T(8,128)(2,1)} %copy.57, bf16[8,64,10,64]{3,0,2,1:T(8,128)(2,1)} %copy.58), kind=kOutput, calls=%fused_computation.12 | convolution fusion | flops 5319680 | bytes 1495040 | tf_op jit(solution)/shard_map/qphd,kphd->phqk/dot_general | solution.py:59
  154.9 1.2 fusion.6
  156.3 2.5 %fusion.5 = bf16[8,64,10,64]{3,0,2,1:T(8,128)(2,1)} fusion(bf16[8,64,10,64]{3,0,2,1:T(8,128)(2,1)S(1)} %copy-done.8, f32[64,10,8,8]{2,3,1,0:T(8,128)S(1)} %get-tuple-element.29, f32[8,64,10]{0,2,1:T(8,128)S(1)} %bitcast.78, f32[64,10,8]{2,1,0:T(8,128)S(1)} %get-tuple-element.28), kind=kOutput, calls=%fused_computation.10 | convolution fusion | flops 6021120 | bytes 1515520 | tf_op jit(solution)/shard_map/phqk,kphd->qphd/dot_general | solution.py:65
  158.8 2.0 %copy.61 = bf16[8,64,10,64]{1,3,2,0:T(8,128)(2,1)S(1)} copy(bf16[8,64,10,64]{3,0,2,1:T(8,128)(2,1)} %fusion.5) | data formatting | bytes 1310720 | tf_op jit(solution)/shard_map/convert_element_type | solution.py:67
  160.8 0.6 copy.62
  161.4 20.6 %all_to_all.9 = bf16[8,64,640]{2,1,0:T(8,128)(2,1)S(1)} all-to-all(bf16[8,64,640]{2,1,0:T(8,128)(2,1)S(1)} %copy.62), channel_id=1, replica_groups=mesh['groups'=2,'frame'=8,'row'=2] {'frame'}, dimensions={0} | all-to-all | bytes 1310720 | tf_op jit(solution)/shard_map/all_to_all | solution.py:136
  182.0 3.3 %convolution_add_fusion = f32[512,640]{1,0:T(8,128)} fusion(f32[512,640]{1,0:T(8,128)} %copy-done.3, bf16[512,640]{1,0:T(8,128)(2,1)S(1)} %bitcast.70, bf16[640,640]{1,0:T(8,128)(2,1)S(1)} %copy-done.10), kind=kOutput, calls=%fused_computation.16 | convolution fusion | flops 419758080 | bytes 4096000 | tf_op jit(solution)/shard_map/dot_general | solution.py:72
  (43 shorter events, 1.1 us)
Async XLA Ops:
  6.5 65.3 %copy-start = (bf16[640,1920]{1,0:T(8,128)(2,1)S(1)}, bf16[640,1920]{1,0:T(8,128)(2,1)}, u32[]{:S(2)}) copy-start(bf16[640,1920]{1,0:T(8,128)(2,1)} %param.13) | copy-start | bytes 7372804
  6.5 75.3 %all-gather.3.cloned.1.call-start = ((), (), s32[]{:S(2)}) async-start(), calls=%async_computation.2 | async-start | bytes 1966080 | tf_op jit(solution)/shard_map/all_gather | solution.py:112
  6.5 58.0 %collective-permute-start = (bf16[1,8,64,640]{3,2,1,0:T(8,128)(2,1)}, bf16[1,8,64,640]{3,2,1,0:T(8,128)(2,1)S(1)}, u32[]{:S(2)}, u32[]{:S(2)}) collective-permute-start(bf16[1,8,64,640]{3,2,1,0:T(8,128)(2,1)} %param.9), channel_id=1, source_target_pairs={{0,2},{2,4},{4,6},{6,8},{8,10},{10,12},{12,14},{1,3},{3,5},{5,7},{... | collective-permute-start | bytes 1966088 | tf_op jit(solution)/shard_map/ppermute | solution.py:16
  11.6 52.9 %collective-permute-start.1 = (bf16[1,8,64,640]{3,2,1,0:T(8,128)(2,1)}, bf16[1,8,64,640]{3,2,1,0:T(8,128)(2,1)}, u32[]{:S(2)}, u32[]{:S(2)}) collective-permute-start(bf16[1,8,64,640]{3,2,1,0:T(8,128)(2,1)} %param.9), channel_id=1, source_target_pairs={{2,0},{4,2},{6,4},{8,6},{10,8},{12,10},{14,12},{3,1},{5,3},{7,5},{... | collective-permute-start | bytes 1966088 | tf_op jit(solution)/shard_map/ppermute | solution.py:19
  67.0 1.7 copy-start.7
  69.5 1.1 copy-start.6
  70.6 1.3 copy-start.12
  71.5 2.2 %copy-start.4 = (f32[512,640]{1,0:T(8,128)}, f32[512,640]{1,0:T(8,128)S(1)}, u32[]{:S(2)}) copy-start(f32[512,640]{1,0:T(8,128)S(1)} %get-tuple-element.23) | copy-start | bytes 3932164
  75.0 19.1 %all-gather.5.cloned.1.call-start = ((), (), s32[]{:S(2)}) async-start(), calls=%async_computation.3 | async-start | bytes 1966080 | tf_op jit(solution)/shard_map/all_gather | solution.py:113
  86.5 7.6 %copy-start.2 = (f32[10,512,1024]{2,1,0:T(8,128)}, f32[10,512,1024]{2,1,0:T(8,128)S(1)}, u32[]{:S(2)}) copy-start(f32[10,512,1024]{2,1,0:T(8,128)S(1)} %get-tuple-element.25) | copy-start | bytes 62914564
  95.7 9.4 %copy-start.5 = (f32[512,640]{1,0:T(8,128)S(1)}, f32[512,640]{1,0:T(8,128)}, u32[]{:S(2)}) copy-start(f32[512,640]{1,0:T(8,128)} %copy-done.4) | copy-start | bytes 3932164
  95.8 9.4 %copy-start.9 = (bf16[640,640]{1,0:T(8,128)(2,1)S(1)}, bf16[640,640]{1,0:T(8,128)(2,1)}, u32[]{:S(2)}) copy-start(bf16[640,640]{1,0:T(8,128)(2,1)} %param.14) | copy-start | bytes 2457604
  105.2 1.2 copy-start.11
  106.1 2.6 %copy-start.3 = (f32[512,640]{1,0:T(8,128)}, f32[512,640]{1,0:T(8,128)S(1)}, u32[]{:S(2)}) copy-start(f32[512,640]{1,0:T(8,128)S(1)} %get-tuple-element.27) | copy-start | bytes 3932164
  154.9 1.3 copy-start.8
  160.8 21.2 %copy-start.10 = (bf16[640,640]{1,0:T(8,128)(2,1)S(1)}, bf16[640,640]{1,0:T(8,128)(2,1)}, u32[]{:S(2)}) copy-start(bf16[640,640]{1,0:T(8,128)(2,1)} %param.17) | copy-start | bytes 2457604
  182.0 3.3 %copy-start.1 = (bf16[640,1920]{1,0:T(8,128)(2,1)S(1)}, bf16[640,1920]{1,0:T(8,128)(2,1)}, u32[]{:S(2)}) copy-start(bf16[640,1920]{1,0:T(8,128)(2,1)} %param.13) | copy-start | bytes 7372804
Sparse Core Ops, SparseCore 0:
  75.1 6.6 all-gather.2
  83.4 10.5 all-gather.4
where the time goes:
time: 193 us; the launch traced here: 192 us
  blocking collectives  93.8 us (49%)
  matrix products  29.7 us (15%)
  local copies, waits for them, and re-layouts  25.7 us (13%)
  other arithmetic  16.2 us (8%)
  between operations  13.8 us (7%)
  starting transfers between devices  6.55 us (3%)
  waiting for transfers between devices  6.39 us (3%)
    psum x1, blocking collectives, body(): first, second = lax.psum((first, second), ('frame', 'row'))  49.5 us
    all_to_all x1, blocking collectives, body(): lax.all_to_all(normed, 'frame', split_axis=1, concat_axis=0, tiled=True)  23.7 us
    all_to_all x1, blocking collectives, body(): lax.all_to_all(result, 'frame', split_axis=0, concat_axis=1, tiled=True)  20.6 us
    unnamed x32, local copies, waits for them, and re-layouts  9.47 us
    dot_general x1, matrix products, body(): jnp.einsum('fhqk,fkhd->fhqd', weights, value_heads, preferred_element_typ...  9.35 us
    all_gather x1, waiting for transfers between devices, body(): key_piece = lax.all_gather(key_rows, 'row', axis=1, tiled=True)  6.1 us
    unnamed x1, other arithmetic  5.57 us
    dot_general x2, matrix products, project_three(): jnp.dot(inputs.reshape(-1, channels), weight, preferred_element_type=jnp....  5.31 us
  transfers between devices with their start and end apart: 4, of which 1 were waited for; matrix products, arithmetic and copies ran while one was open for 6% of the time, Pallas kernels for 0%

commit v1 on v0

--- a/solution.py
+++ b/solution.py
@@ -6,6 +6,17 @@
 HEADS = 10
 GROUPS = 32
 epsilon = 1e-05
+
+
+def in_blocks(array, dim, length):
+    before, after = (array.shape[:dim], array.shape[dim + 1 :])
+    return jnp.moveaxis(array.reshape(*before, length, -1, *after), dim, 0)
+
+
+def laid_out(blocks, dim):
+    dims = list(blocks.shape[1:])
+    dims[dim] *= blocks.shape[0]
+    return jnp.moveaxis(blocks, 0, dim).reshape(dims)
 
 
 def padded_2(block, sides, width):
@@ -130,7 +141,14 @@
     attended = jnp.transpose(attended, (0, 2, 1, 3)).reshape(frames, pixels, channels)
     spaced = add_projected(stepped, attended, space_out)
     normed = layer_norm(spaced, time_norm)
-    moved = lax.all_to_all(normed, "frame", split_axis=1, concat_axis=0, tiled=True)
+    size, index = (lax.axis_size("frame"), lax.axis_index("frame"))
+    pieces = in_blocks(normed, 1, size)
+    outs = [pieces[index]]
+    for turn in range(1, size):
+        sent = pieces[index ^ turn]
+        outs.append(lax.ppermute(sent, "frame", [(i_2, i_2 ^ turn) for i_2 in range(size)]))
+    pieces = jnp.stack(outs)[index ^ jnp.arange(size)]
+    moved = laid_out(pieces, 0)
     queries, key_rows, values = project_three(moved, time_qkv)
     result = time_attend(queries, key_rows, values)
     result = lax.all_to_all(result, "frame", split_axis=0, concat_axis=1, tiled=True)

time: 193 us -> 183 us (0.948)
  blocking collectives: 93.8 us -> 72.7 us
  starting transfers between devices: 6.55 us -> 17.6 us
  waiting for transfers between devices: 6.39 us -> 14.7 us
  other arithmetic: 16.2 us -> 10.7 us
  local copies, waits for them, and re-layouts: 25.7 us -> 23.6 us
    all_to_all x1 -> x0, blocking collectives: 23.7 us -> none  [body(): lax.all_to_all(normed, 'frame', split_axis=1, concat_axis=0, tiled=True)]
    ppermute x0 -> x7, starting transfers between devices: none -> 11.2 us  [body(): lax.ppermute(sent, 'frame', [(i_2, i_2 ^ turn) for i_2 in range(size)])]
    ppermute x0 -> x7, waiting for transfers between devices: none -> 8.22 us  [body(): lax.ppermute(sent, 'frame', [(i_2, i_2 ^ turn) for i_2 in range(size)])]
    unnamed x1 -> x0, other arithmetic: 5.57 us -> none
    all_to_all x1, blocking collectives: 20.6 us -> 23.2 us  [body(): lax.all_to_all(result, 'frame', split_axis=0, concat_axis=1, tiled=True)]
    convert_element_type x1 -> x0, local copies, waits for them, and re-layouts: 2.07 us -> none  [layer_norm(): return (shifted * lax.rsqrt(spread + epsilon) * gain).astype(jnp.bfloat16)]
    unnamed x32 -> x35, local copies, waits for them, and re-layouts: 9.47 us -> 8.62 us
  transfers between devices with their start and end apart: 4 -> 11, of which waited for: 1 -> 2; matrix products, arithmetic and copies ran while one was open for 6% -> 6% of each run, Pallas kernels for 0% -> 0%
where the time goes in v1:
time: 183 us
  blocking collectives  72.7 us (40%)
  matrix products  29.4 us (16%)
  local copies, waits for them, and re-layouts  23.6 us (13%)
  starting transfers between devices  17.6 us (10%)
  waiting for transfers between devices  14.7 us (8%)
  between operations  13.9 us (8%)
  other arithmetic  10.7 us (6%)
    psum x1, blocking collectives, body(): first, second = lax.psum((first, second), ('frame', 'row'))  49.5 us
    all_to_all x1, blocking collectives, body(): lax.all_to_all(result, 'frame', split_axis=0, concat_axis=1, tiled=True)  23.2 us
    ppermute x7, starting transfers between devices, body(): lax.ppermute(sent, 'frame', [(i_2, i_2 ^ turn) for i_2 in range(size)])  11.2 us
    dot_general x1, matrix products, body(): jnp.einsum('fhqk,fkhd->fhqd', weights, value_heads, preferred_element_typ...  9.13 us
    unnamed x35, local copies, waits for them, and re-layouts  8.62 us
    ppermute x7, waiting for transfers between devices, body(): lax.ppermute(sent, 'frame', [(i_2, i_2 ^ turn) for i_2 in range(size)])  8.22 us
    all_gather x1, waiting for transfers between devices, body(): key_piece = lax.all_gather(key_rows, 'row', axis=1, tiled=True)  6.1 us
    dot_general x2, matrix products, project_three(): jnp.dot(inputs.reshape(-1, channels), weight, preferred_element_type=jnp....  5.31 us
  transfers between devices with their start and end apart: 11, of which 2 were waited for; matrix products, arithmetic and copies ran while one was open for 6% of the time, Pallas kernels for 0%

profile of v1, /device:TPU:0, one launch (start us, length us, event | category | flops | bytes accessed | tf_op | source)
XLA Modules:
  0.0 182.6 jit_solution(16572023374346034298)
XLA Ops:
  6.5 5.0 %collective-permute-start = (bf16[1,8,64,640]{3,2,1,0:T(8,128)(2,1)}, bf16[1,8,64,640]{3,2,1,0:T(8,128)(2,1)S(1)}, u32[]{:S(2)}, u32[]{:S(2)}) collective-permute-start(bf16[1,8,64,640]{3,2,1,0:T(8,128)(2,1)} %param.9), channel_id=1, source_target_pairs={{0,2},{2,4},{4,6},{6,8},{8,10},{10,12},{12,14},{1,3},{3,5},{5,7},{... | collective-permute-start | bytes 1966088 | tf_op jit(solution)/shard_map/ppermute | solution.py:27
  11.6 1.3 collective-permute-start.1
  12.9 1.3 convert_reduce_fusion
  14.6 49.5 %all-reduce = (f32[32]{0:T(128)S(1)}, f32[32]{0:T(128)S(1)}) all-reduce(f32[32]{0:T(128)S(1)} %reduce_sum.91, f32[32]{0:T(128)S(1)} %reduce_sum.88), channel_id=1, replica_groups=mesh['groups'=2,'frame'=8,'row'=2] {'frame','row'}, use_global_device_ids=true, to_apply=%region_5.6 | all-reduce | flops 64 | bytes 512 | tf_op jit(solution)/shard_map/psum | solution.py:99
  64.5 2.5 %fusion.8 = bf16[3,8,64,640]{3,2,1,0:T(8,128)(2,1)S(1)} fusion(bf16[1,8,64,640]{3,2,1,0:T(8,128)(2,1)} %collective-permute-done.1, bf16[1,8,64,640]{3,2,1,0:T(8,128)(2,1)} %param.9, bf16[1,8,64,640]{3,2,1,0:T(8,128)(2,1)S(1)} %collective-permute-done, f32[640]{0:T(1024)} %param.10, f32[640]{0:T(1024)S(1)} %mul.99, f32[640]{0:T(1024)S(1)} %sub.69, ...), kind=kLoop, calls=%fused_computation.16 | loop fusion | flops 11796480 | bytes 3939843 | tf_op jit(solution)/shard_map/jit(_where)/select_n | solution.py:110
  67.3 1.5 copy-done.7
  68.7 0.8 fusion.19
  69.5 0.7 fusion.21
  70.3 0.3 copy-done.6
  70.6 0.9 fusion.37
  71.6 0.3 multiply_reduce_fusion.3
  71.9 1.9 %fusion.4 = bf16[1,512,1920]{2,1,0:T(8,128)(2,1)S(1)} fusion(bf16[640,1920]{1,0:T(8,128)(2,1)S(1)} %copy-done, f32[512,640]{1,0:T(8,128)S(1)} %get-tuple-element.31, f32[640]{0:T(1024)S(1)} %copy-done.12, f32[512]{0:T(512)S(1)} %add_rsqrt_fusion.1, f32[512]{0:T(512)S(1)} %broadcast_multiply_fusion.1), kind=kOutput, calls=%fused_computation.9 | convolution fusion | flops 1260584960 | bytes 5741056 | tf_op jit(solution)/shard_map/dot_general | solution.py:53
  73.8 1.2 fusion.35
  75.4 0.4 all-gather.5.cloned.1.call-update
  75.8 6.1 %all-gather.3.cloned.1.call-done = bf16[1,1024,640]{2,1,0:T(8,128)(2,1)} async-done(((bf16[1,512,640]{2,1,0:T(8,128)(2,1)}), bf16[1,1024,640]{2,1,0:T(8,128)(2,1)}) %all-gather.3.cloned.1.call-update) | async-done | bytes 1310736 | tf_op jit(solution)/shard_map/all_gather | solution.py:123
  81.9 1.6 copy.38
  83.5 3.0 %multiply_reduce_fusion = (f32[10,512]{1,0:T(8,128)S(1)}, f32[10,512,1024]{2,1,0:T(8,128)S(1)}) fusion(bf16[512,10,64]{0,2,1:T(8,128)(2,1)S(1)} %bitcast.93, bf16[1024,10,64]{0,2,1:T(8,128)(2,1)S(1)} %bitcast.88), kind=kOutput, calls=%fused_computation.2 | convolution fusion | flops 681569280 | bytes 22958080 | tf_op jit(solution)/shard_map/fqhd,fkhd->fhqk/dot_general | solution.py:128
  86.5 4.6 %fusion = f32[10,512]{1,0:T(8,128)S(1)} fusion(f32[10,512,1024]{2,1,0:T(8,128)S(1)} %get-tuple-element.33, f32[10,512]{1,0:T(8,128)S(1)} %get-tuple-element.32), kind=kLoop, calls=%fused_computation.3 | loop fusion | flops 15723520 | bytes 21012480 | tf_op jit(solution)/shard_map/reduce_sum | solution.py:134
  91.1 3.0 %copy-done.2 = f32[10,512,1024]{2,1,0:T(8,128)} copy-done((f32[10,512,1024]{2,1,0:T(8,128)}, f32[10,512,1024]{2,1,0:T(8,128)S(1)}, u32[]{:S(2)}) %copy-start.2) | copy-done | bytes 20971544
  94.1 1.6 copy.39
  95.8 9.1 %divide_convert_fusion = bf16[10,512,64]{1,2,0:T(8,128)(2,1)S(1)} fusion(bf16[1024,10,64]{0,2,1:T(8,128)(2,1)S(1)} %bitcast.100, f32[10,512,1024]{2,1,0:T(8,128)} %copy-done.2, f32[10,512]{1,0:T(8,128)S(1)} %get-tuple-element.32, f32[10,512]{1,0:T(8,128)S(1)} %get-tuple-element.27, f32[10,512]{1,0:T(8,128)S(1)} %get-tuple-element.26), kind=kOutput, calls=%fused_computation.27 | convolution fusion | flops 687800320 | bytes 22999040 | tf_op jit(solution)/shard_map/fhqk,fkhd->fhqd/dot_general | solution.py:136
  105.0 0.9 fusion.38
  105.9 0.3 multiply_reduce_fusion.2
  106.5 0.4 copy-done.3
  106.9 1.7 collective-permute-start.2
  108.7 1.5 collective-permute-start.3
  110.2 0.3 collective-permute-start.4
  110.4 2.7 %collective-permute-start.5 = (bf16[1,64,640]{2,1,0:T(8,128)(2,1)S(1)}, bf16[1,64,640]{2,1,0:T(8,128)(2,1)S(1)}, u32[]{:S(2)}, u32[]{:S(2)}) collective-permute-start(bf16[1,64,640]{2,1,0:T(8,128)(2,1)S(1)} %get-tuple-element.21), channel_id=1, source_target_pairs={{0,8},{2,10},{4,12},{6,14},{8,0},{10,2},{12,4},{14,6},{1,9},{3,11}... | collective-permute-start | bytes 245768 | tf_op jit(solution)/shard_map/ppermute | solution.py:149
  113.1 1.4 collective-permute-start.6
  114.5 3.3 %collective-permute-start.7 = (bf16[1,64,640]{2,1,0:T(8,128)(2,1)S(1)}, bf16[1,64,640]{2,1,0:T(8,128)(2,1)S(1)}, u32[]{:S(2)}, u32[]{:S(2)}) collective-permute-start(bf16[1,64,640]{2,1,0:T(8,128)(2,1)S(1)} %get-tuple-element.19), channel_id=1, source_target_pairs={{0,12},{2,14},{4,8},{6,10},{8,4},{10,6},{12,0},{14,2},{1,13},{3,15... | collective-permute-start | bytes 245768 | tf_op jit(solution)/shard_map/ppermute | solution.py:149
  117.9 0.3 collective-permute-start.8
  118.2 8.2 %collective-permute-done.6 = bf16[1,64,640]{2,1,0:T(8,128)(2,1)S(1)} collective-permute-done((bf16[1,64,640]{2,1,0:T(8,128)(2,1)S(1)}, bf16[1,64,640]{2,1,0:T(8,128)(2,1)S(1)}, u32[]{:S(2)}, u32[]{:S(2)}) %collective-permute-start.6) | collective-permute-done | bytes 81952 | tf_op jit(solution)/shard_map/ppermute | solution.py:149
  126.5 0.7 gather_fusion
  127.2 3.4 %convolution_convert_fusion = bf16[512,1920]{1,0:T(8,128)(2,1)S(1)} fusion(bf16[512,640]{1,0:T(8,128)(2,1)S(1)} %bitcast.103, bf16[640,1920]{1,0:T(8,128)(2,1)} %param.16), kind=kOutput, calls=%fused_computation.7 | convolution fusion | flops 1259274240 | bytes 5079040 | tf_op jit(solution)/shard_map/dot_general | solution.py:53
  130.6 1.1 fusion.34
  131.8 1.6 copy.51
  133.4 1.7 copy.43
  135.1 0.8 copy.52
  135.9 1.6 copy.44
  137.5 0.8 copy.50
  138.2 1.7 copy.45
  139.9 2.8 %multiply_reduce_fusion.1 = (f32[64,10,8]{2,1,0:T(8,128)S(1)}, f32[64,10,8,8]{2,3,1,0:T(8,128)S(1)}) fusion(bf16[8,64,10,64]{3,0,2,1:T(8,128)(2,1)} %copy.43, bf16[8,64,10,64]{3,0,2,1:T(8,128)(2,1)} %copy.44), kind=kOutput, calls=%fused_computation.13 | convolution fusion | flops 5319680 | bytes 1495040 | tf_op jit(solution)/shard_map/qphd,kphd->phqk/dot_general | solution.py:70
  142.8 1.2 fusion.6
  144.1 2.5 %fusion.5 = bf16[8,64,10,64]{3,0,2,1:T(8,128)(2,1)} fusion(bf16[8,64,10,64]{3,0,2,1:T(8,128)(2,1)S(1)} %copy-done.8, f32[64,10,8,8]{2,3,1,0:T(8,128)S(1)} %get-tuple-element.37, f32[8,64,10]{0,2,1:T(8,128)S(1)} %bitcast.104, f32[64,10,8]{2,1,0:T(8,128)S(1)} %get-tuple-element.36), kind=kOutput, calls=%fused_computation.11 | convolution fusion | flops 6021120 | bytes 1515520 | tf_op jit(solution)/shard_map/phqk,kphd->qphd/dot_general | solution.py:76
  146.6 2.0 %copy.47 = bf16[8,64,10,64]{1,3,2,0:T(8,128)(2,1)S(1)} copy(bf16[8,64,10,64]{3,0,2,1:T(8,128)(2,1)} %fusion.5) | data formatting | bytes 1310720 | tf_op jit(solution)/shard_map/convert_element_type | solution.py:78
  148.6 0.6 copy.48
  149.3 23.2 %all_to_all.4 = bf16[8,64,640]{2,1,0:T(8,128)(2,1)S(1)} all-to-all(bf16[8,64,640]{2,1,0:T(8,128)(2,1)S(1)} %copy.48), channel_id=1, replica_groups=mesh['groups'=2,'frame'=8,'row'=2] {'frame'}, dimensions={0} | all-to-all | bytes 1310720 | tf_op jit(solution)/shard_map/all_to_all | solution.py:154
  172.5 3.3 %convolution_add_fusion = f32[512,640]{1,0:T(8,128)} fusion(f32[512,640]{1,0:T(8,128)} %copy-done.3, bf16[512,640]{1,0:T(8,128)(2,1)S(1)} %bitcast.94, bf16[640,640]{1,0:T(8,128)(2,1)S(1)} %copy-done.10), kind=kOutput, calls=%fused_computation.17 | convolution fusion | flops 419758080 | bytes 4096000 | tf_op jit(solution)/shard_map/dot_general | solution.py:83
  (62 shorter events, 2.0 us)
Async XLA Ops:
  6.5 65.3 %copy-start = (bf16[640,1920]{1,0:T(8,128)(2,1)S(1)}, bf16[640,1920]{1,0:T(8,128)(2,1)}, u32[]{:S(2)}) copy-start(bf16[640,1920]{1,0:T(8,128)(2,1)} %param.13) | copy-start | bytes 7372804
  6.5 75.3 %all-gather.3.cloned.1.call-start = ((), (), s32[]{:S(2)}) async-start(), calls=%async_computation.1 | async-start | bytes 1966080 | tf_op jit(solution)/shard_map/all_gather | solution.py:123
  6.5 58.0 %collective-permute-start = (bf16[1,8,64,640]{3,2,1,0:T(8,128)(2,1)}, bf16[1,8,64,640]{3,2,1,0:T(8,128)(2,1)S(1)}, u32[]{:S(2)}, u32[]{:S(2)}) collective-permute-start(bf16[1,8,64,640]{3,2,1,0:T(8,128)(2,1)} %param.9), channel_id=1, source_target_pairs={{0,2},{2,4},{4,6},{6,8},{8,10},{10,12},{12,14},{1,3},{3,5},{5,7},{... | collective-permute-start | bytes 1966088 | tf_op jit(solution)/shard_map/ppermute | solution.py:27
  11.6 52.9 %collective-permute-start.1 = (bf16[1,8,64,640]{3,2,1,0:T(8,128)(2,1)}, bf16[1,8,64,640]{3,2,1,0:T(8,128)(2,1)}, u32[]{:S(2)}, u32[]{:S(2)}) collective-permute-start(bf16[1,8,64,640]{3,2,1,0:T(8,128)(2,1)} %param.9), channel_id=1, source_target_pairs={{2,0},{4,2},{6,4},{8,6},{10,8},{12,10},{14,12},{3,1},{5,3},{7,5},{... | collective-permute-start | bytes 1966088 | tf_op jit(solution)/shard_map/ppermute | solution.py:30
  67.0 1.7 copy-start.7
  69.5 1.1 copy-start.6
  70.6 1.3 copy-start.12
  71.5 2.2 %copy-start.4 = (f32[512,640]{1,0:T(8,128)}, f32[512,640]{1,0:T(8,128)S(1)}, u32[]{:S(2)}) copy-start(f32[512,640]{1,0:T(8,128)S(1)} %get-tuple-element.31) | copy-start | bytes 3932164
  75.0 19.1 %all-gather.5.cloned.1.call-start = ((), (), s32[]{:S(2)}) async-start(), calls=%async_computation.2 | async-start | bytes 1966080 | tf_op jit(solution)/shard_map/all_gather | solution.py:124
  86.5 7.6 %copy-start.2 = (f32[10,512,1024]{2,1,0:T(8,128)}, f32[10,512,1024]{2,1,0:T(8,128)S(1)}, u32[]{:S(2)}) copy-start(f32[10,512,1024]{2,1,0:T(8,128)S(1)} %get-tuple-element.33) | copy-start | bytes 62914564
  95.8 9.2 %copy-start.5 = (f32[512,640]{1,0:T(8,128)S(1)}, f32[512,640]{1,0:T(8,128)}, u32[]{:S(2)}) copy-start(f32[512,640]{1,0:T(8,128)} %copy-done.4) | copy-start | bytes 3932164
  95.8 9.2 %copy-start.9 = (bf16[640,640]{1,0:T(8,128)(2,1)S(1)}, bf16[640,640]{1,0:T(8,128)(2,1)}, u32[]{:S(2)}) copy-start(bf16[640,640]{1,0:T(8,128)(2,1)} %param.14) | copy-start | bytes 2457604
  104.9 1.2 copy-start.11
  105.9 1.1 copy-start.3
  106.9 7.6 %collective-permute-start.2 = (bf16[1,64,640]{2,1,0:T(8,128)(2,1)S(1)}, bf16[1,64,640]{2,1,0:T(8,128)(2,1)S(1)}, u32[]{:S(2)}, u32[]{:S(2)}) collective-permute-start(bf16[1,64,640]{2,1,0:T(8,128)(2,1)S(1)} %get-tuple-element.24), channel_id=1, source_target_pairs={{0,2},{2,0},{4,6},{6,4},{8,10},{10,8},{12,14},{14,12},{1,3},{3,1},... | collective-permute-start | bytes 245768 | tf_op jit(solution)/shard_map/ppermute | solution.py:149
  108.7 9.2 %collective-permute-start.3 = (bf16[1,64,640]{2,1,0:T(8,128)(2,1)S(1)}, bf16[1,64,640]{2,1,0:T(8,128)(2,1)S(1)}, u32[]{:S(2)}, u32[]{:S(2)}) collective-permute-start(bf16[1,64,640]{2,1,0:T(8,128)(2,1)S(1)} %get-tuple-element.23), channel_id=1, source_target_pairs={{0,4},{2,6},{4,0},{6,2},{8,12},{10,14},{12,8},{14,10},{1,5},{3,7},... | collective-permute-start | bytes 245768 | tf_op jit(solution)/shard_map/ppermute | solution.py:149
  110.2 8.0 %collective-permute-start.4 = (bf16[1,64,640]{2,1,0:T(8,128)(2,1)S(1)}, bf16[1,64,640]{2,1,0:T(8,128)(2,1)S(1)}, u32[]{:S(2)}, u32[]{:S(2)}) collective-permute-start(bf16[1,64,640]{2,1,0:T(8,128)(2,1)S(1)} %get-tuple-element.22), channel_id=1, source_target_pairs={{0,6},{2,4},{4,2},{6,0},{8,14},{10,12},{12,10},{14,8},{1,7},{3,5},... | collective-permute-start | bytes 245768 | tf_op jit(solution)/shard_map/ppermute | solution.py:149
  110.4 7.8 %collective-permute-start.5 = (bf16[1,64,640]{2,1,0:T(8,128)(2,1)S(1)}, bf16[1,64,640]{2,1,0:T(8,128)(2,1)S(1)}, u32[]{:S(2)}, u32[]{:S(2)}) collective-permute-start(bf16[1,64,640]{2,1,0:T(8,128)(2,1)S(1)} %get-tuple-element.21), channel_id=1, source_target_pairs={{0,8},{2,10},{4,12},{6,14},{8,0},{10,2},{12,4},{14,6},{1,9},{3,11}... | collective-permute-start | bytes 245768 | tf_op jit(solution)/shard_map/ppermute | solution.py:149
  113.1 13.3 %collective-permute-start.6 = (bf16[1,64,640]{2,1,0:T(8,128)(2,1)S(1)}, bf16[1,64,640]{2,1,0:T(8,128)(2,1)S(1)}, u32[]{:S(2)}, u32[]{:S(2)}) collective-permute-start(bf16[1,64,640]{2,1,0:T(8,128)(2,1)S(1)} %get-tuple-element.20), channel_id=1, source_target_pairs={{0,10},{2,8},{4,14},{6,12},{8,2},{10,0},{12,6},{14,4},{1,11},{3,9}... | collective-permute-start | bytes 245768 | tf_op jit(solution)/shard_map/ppermute | solution.py:149
  114.5 11.9 %collective-permute-start.7 = (bf16[1,64,640]{2,1,0:T(8,128)(2,1)S(1)}, bf16[1,64,640]{2,1,0:T(8,128)(2,1)S(1)}, u32[]{:S(2)}, u32[]{:S(2)}) collective-permute-start(bf16[1,64,640]{2,1,0:T(8,128)(2,1)S(1)} %get-tuple-element.19), channel_id=1, source_target_pairs={{0,12},{2,14},{4,8},{6,10},{8,4},{10,6},{12,0},{14,2},{1,13},{3,15... | collective-permute-start | bytes 245768 | tf_op jit(solution)/shard_map/ppermute | solution.py:149
  117.9 8.6 %collective-permute-start.8 = (bf16[1,64,640]{2,1,0:T(8,128)(2,1)S(1)}, bf16[1,64,640]{2,1,0:T(8,128)(2,1)S(1)}, u32[]{:S(2)}, u32[]{:S(2)}) collective-permute-start(bf16[1,64,640]{2,1,0:T(8,128)(2,1)S(1)} %get-tuple-element.18), channel_id=1, source_target_pairs={{0,14},{2,12},{4,10},{6,8},{8,6},{10,4},{12,2},{14,0},{1,15},{3,13... | collective-permute-start | bytes 245768 | tf_op jit(solution)/shard_map/ppermute | solution.py:149
  142.8 1.3 copy-start.8
  148.6 23.8 %copy-start.10 = (bf16[640,640]{1,0:T(8,128)(2,1)S(1)}, bf16[640,640]{1,0:T(8,128)(2,1)}, u32[]{:S(2)}) copy-start(bf16[640,640]{1,0:T(8,128)(2,1)} %param.17) | copy-start | bytes 2457604
  172.5 3.3 %copy-start.1 = (bf16[640,1920]{1,0:T(8,128)(2,1)S(1)}, bf16[640,1920]{1,0:T(8,128)(2,1)}, u32[]{:S(2)}) copy-start(bf16[640,1920]{1,0:T(8,128)(2,1)} %param.13) | copy-start | bytes 7372804
Sparse Core Ops, SparseCore 0:
  75.1 6.6 all-gather.2
  83.4 10.5 all-gather.4
